TPU v7x, 256 devices: a whole 4x4x8 slice. The times are simulated.
256 devices in a mesh: grp: 2 (over core), dev: 128 (over x, y, z).
Axes of the slice: x: 4, y: 4, z: 8, core: 2. Of those that a mesh axis runs over, the one named last changes fastest.
Arguments:
- coarse_emb: bfloat16 [131072, 128], P('dev'), may hold values from -6 to 6
- req_ids: int32 [128, 2, 128, 16], P('dev', 'grp'), may hold values from 0 to 1023, as said below
- fine_slot: int32 [128, 2, 2048], P('dev', 'grp'), may hold values from 0 to 2047, as said below
- tiles: bfloat16 [4096, 2, 8, 128, 128], P('dev', 'grp'), may hold values from -0.125 to 0.125
- tile_cols: int32 [4096, 2, 8], P('dev', 'grp'), may hold values from 0 to 47
Outputs:
- smoothed: bfloat16 [524288, 128], P('dev')
Inputs may be any that keep to these rules, and one draw needn't show every extreme that they name: For each d, g and o only the first entries of req_ids[d, g, o] are requested, at most 16 of them, and for each d and g some owner o has all 16; the remaining entries are 0. fine_slot[d, g, i] = o * 16 + j always names a requested entry j of req_ids[d, g, o], and every requested entry is named by some fine node.
All inputs are finite; a program needn't handle non-finite values.
Results may differ from a plain program's by a relative error of at most 0.001.
Values may be sent and summed in bfloat16 or wider, within the bound.
No kernel may reach another device: no remote copies, remote signals or barrier semaphores. Data moves between devices by JAX's collectives and lax.ppermute only.
A program may use at most 64 MiB of HBM per device.

v0:
```python
import jax
import jax.numpy as jnp
from jax import lax
from jax.sharding import PartitionSpec as P


def with_halo(shard, sides, width):
    for axis, dim in sides:
        count, length = (lax.axis_size(axis), shard.shape[dim])
        up = [(i, (i + 1) % count) for i in range(count - 1)]
        down = [(j, i) for i, j in up]
        last = lax.slice_in_dim(shard, length - width, length, axis=dim)
        initial = lax.slice_in_dim(shard, 0, width, axis=dim)
        before = lax.ppermute(last, axis, up)
        after = lax.ppermute(initial, axis, down)
        shard = jnp.concatenate([before, shard, after], axis=dim)
    return shard


def per_device(coarse_emb, req_ids, fine_slot, tiles, tile_cols):
    owners = lax.axis_size("dev")
    slot_count = req_ids.shape[3]
    feature_dim = coarse_emb.shape[1]
    half_rows = fine_slot.shape[2]
    tile_rows = tiles.shape[3]
    fine_rows = tiles.shape[0] * tile_rows
    wanted_rows = jnp.take(
        coarse_emb, lax.all_to_all(req_ids, "dev", split_axis=2, concat_axis=0, tiled=True), axis=0
    )
    received = lax.all_to_all(wanted_rows, "dev", split_axis=0, concat_axis=2, tiled=True)
    slot_table = received.reshape(owners * slot_count, feature_dim)
    rows_per = min(512, half_rows)
    block_count = half_rows // rows_per
    columns = lax.iota(jnp.int32, owners * slot_count)

    def lift_block(slot_block):
        onehot = (slot_block[:, None] == columns[None, :]).astype(jnp.bfloat16)
        return jnp.dot(onehot, slot_table, preferred_element_type=jnp.float32).astype(jnp.bfloat16)

    lifted = lax.map(lift_block, fine_slot.reshape(block_count, rows_per)).reshape(
        half_rows, feature_dim
    )
    extended = with_halo(lifted, (("dev", 0),), half_rows)
    ext_blocks = extended.reshape(3 * half_rows // tile_rows, tile_rows, feature_dim)
    picked = ext_blocks[tile_cols[:, 0, :]]
    tile_sums = jnp.einsum(
        "rtij,rtjw->riw", tiles[:, 0], picked, preferred_element_type=jnp.float32
    )
    tile_sums = tile_sums.reshape(fine_rows, feature_dim)
    group = lax.axis_index("grp")
    own_part = lax.dynamic_update_slice(
        jnp.zeros((fine_rows, feature_dim), jnp.float32),
        lifted.astype(jnp.float32),
        (group * half_rows, 0),
    )
    partial_value = own_part - 0.5 * tile_sums
    summed = lax.psum(partial_value, "grp")
    return summed.astype(jnp.bfloat16)


def solution(mesh):
    return jax.shard_map(
        per_device,
        mesh=mesh,
        in_specs=(
            P("dev", None),
            P("dev", "grp", None, None),
            P("dev", "grp", None),
            P("dev", "grp", None, None, None),
            P("dev", "grp", None),
        ),
        out_specs=P("dev", None),
        check_vma=False,
    )
```

profile of v0, /device:TPU:1, one launch (start us, length us, event | category | flops | bytes accessed | tf_op | source)
XLA Modules:
  0.0 108.3 jit_solution(4448812067448210851)
XLA Ops:
  0.0 0.0 copy-start
  0.0 0.8 copy.10
  0.8 26.7 %all_to_all.24 = s32[1,1,128,16]{3,1,0,2:T(1,128)S(1)} all-to-all(s32[1,1,128,16]{3,1,0,2:T(1,128)S(1)} %copy.10), channel_id=1, replica_groups=mesh['grp'=2,'dev'=128] {'dev'}, dimensions={2} | all-to-all | bytes 16384 | tf_op jit(solution)/shard_map/all_to_all | solution.py:28
  27.6 0.1 reshape.137
  27.7 0.0 copy-done
  27.7 0.0 copy-start.3
  27.7 0.0 copy-start.4
  27.7 6.2 %gather_fusion = bf16[2048,128]{1,0:T(8,128)(2,1)S(1)} fusion(bf16[1024,128]{1,0:T(8,128)(2,1)S(1)} %copy-done, s32[2048]{0:T(1024)S(1)} %broadcast_clamp_fusion), kind=kCustom, calls=%fused_computation | custom fusion | bytes 1056768 | tf_op jit(solution)/shard_map/jit(_take)/gather | solution.py:27
  33.9 1.1 %broadcast_select_fusion = bf16[128,1,1,16,128]{4,3,2,1,0:T(8,128)(2,1)} fusion(bf16[128,1,1,16,128]{4,3,2,1,0:T(8,128)(2,1)S(1)} %bitcast.44, pred[128,16]{1,0:T(8,128)(4,1)S(1)} %compare_and_fusion), kind=kLoop, calls=%fused_computation.16 | loop fusion | flops 262144 | bytes 1050624 | tf_op jit(solution)/shard_map/jit(_take)/select_n | solution.py:27
  35.0 6.2 %all-to-all-start.1 = ((bf16[128,1,1,16,128]{4,3,2,1,0:T(8,128)(2,1)}), bf16[128,1,1,16,128]{4,3,2,1,0:T(8,128)(2,1)S(1)}, u32[]{:S(2)}, u32[]{:S(2)}) async-start(bf16[128,1,1,16,128]{4,3,2,1,0:T(8,128)(2,1)} %broadcast_select_fusion), calls=%async_computation.1 | async-start | bytes 1048576 | tf_op jit(solution)/shard_map/all_to_all | solution.py:30
  41.2 0.5 broadcast.89
  41.8 0.6 reduce.3
  42.4 0.1 copy.12
  42.5 0.1 reshape.145
  42.5 17.0 %all-to-all-done.1 = bf16[128,1,1,16,128]{4,3,2,1,0:T(8,128)(2,1)S(1)} async-done(((bf16[128,1,1,16,128]{4,3,2,1,0:T(8,128)(2,1)}), bf16[128,1,1,16,128]{4,3,2,1,0:T(8,128)(2,1)S(1)}, u32[]{:S(2)}, u32[]{:S(2)}) %all-to-all-start.1) | async-done | bytes 524320 | tf_op jit(solution)/shard_map/all_to_all | solution.py:30
  59.5 3.7 %while.11 = (s32[]{:T(128)}, bf16[4,512,128]{2,1,0:T(8,128)(2,1)S(1)}, s32[4,512]{1,0:T(4,128)S(1)}, bf16[2048,128]{1,0:T(8,128)(2,1)S(1)}, s32[]{:T(128)}) while((s32[]{:T(128)}, bf16[4,512,128]{2,1,0:T(8,128)(2,1)S(1)}, s32[4,512]{1,0:T(4,128)S(1)}, bf16[2048,128]{1,0:T(8,128)(2,1)S(1)}, s32[]{:T(128)}) %tuple.24), condition=%wide.region_1.2_spmd.clone, body=%wide.region_0.1_spmd.clone.sunk | while | flops 269549568 | bytes 661573 | solution.py:40
  59.5 0.9 fusion.16
  60.4 0.9 fusion.16
  61.4 0.9 fusion.16
  62.3 0.9 fusion.16
  63.2 2.5 %collective-permute-start = (bf16[2048,128]{1,0:T(8,128)(2,1)S(1)}, bf16[2048,128]{1,0:T(8,128)(2,1)S(1)}, u32[]{:S(2)}, u32[]{:S(2)}) collective-permute-start(bf16[2048,128]{1,0:T(8,128)(2,1)S(1)} %bitcast.45), channel_id=1, source_target_pairs={{0,1},{1,2},{2,3},{3,4},{4,5},{5,6},{6,7},{7,8},{8,9},{9,10},{10,1... | collective-permute-start | bytes 1572872 | tf_op jit(solution)/shard_map/ppermute | solution.py:14
  65.7 1.3 %collective-permute-start.1 = (bf16[2048,128]{1,0:T(8,128)(2,1)S(1)}, bf16[2048,128]{1,0:T(8,128)(2,1)S(1)}, u32[]{:S(2)}, u32[]{:S(2)}) collective-permute-start(bf16[2048,128]{1,0:T(8,128)(2,1)S(1)} %bitcast.46), channel_id=1, source_target_pairs={{1,0},{2,1},{3,2},{4,3},{5,4},{6,5},{7,6},{8,7},{9,8},{10,9},{11,1... | collective-permute-start | bytes 1572872 | tf_op jit(solution)/shard_map/ppermute | solution.py:15
  67.0 0.1 broadcast_in_dim.23
  67.2 0.1 convert_dynamic-update-slice_fusion
  67.3 0.0 copy-start.1
  67.3 6.6 %collective-permute-done = bf16[2048,128]{1,0:T(8,128)(2,1)S(1)} collective-permute-done((bf16[2048,128]{1,0:T(8,128)(2,1)S(1)}, bf16[2048,128]{1,0:T(8,128)(2,1)S(1)}, u32[]{:S(2)}, u32[]{:S(2)}) %collective-permute-start) | collective-permute-done | bytes 524320 | tf_op jit(solution)/shard_map/ppermute | solution.py:14
  73.9 3.9 %collective-permute-done.1 = bf16[2048,128]{1,0:T(8,128)(2,1)S(1)} collective-permute-done((bf16[2048,128]{1,0:T(8,128)(2,1)S(1)}, bf16[2048,128]{1,0:T(8,128)(2,1)S(1)}, u32[]{:S(2)}, u32[]{:S(2)}) %collective-permute-start.1) | collective-permute-done | bytes 524320 | tf_op jit(solution)/shard_map/ppermute | solution.py:15
  77.7 0.1 pad_maximum_fusion
  77.8 8.6 %gather_fusion.1 = bf16[256,128,128]{2,1,0:T(8,128)(2,1)} fusion(bf16[48,128,128]{2,1,0:T(8,128)(2,1)S(1)} %bitcast.42, s32[1024]{0:T(1024)S(1)} %pad_clamp_fusion), kind=kCustom, calls=%fused_computation.1 | custom fusion | bytes 16778240 | tf_op jit(solution)/shard_map/gather | solution.py:45
  86.4 8.3 %bitcast_multiply_fusion = f32[32,128,128]{1,2,0:T(8,128)S(1)} fusion(bf16[32,8,128,128]{3,2,1,0:T(8,128)(2,1)} %bitcast.43, bf16[32,1,8,128,128]{4,3,2,1,0:T(8,128)(2,1)} %param.10), kind=kOutput, calls=%fused_computation.13 | convolution fusion | flops 1074266112 | bytes 18874368 | tf_op jit(solution)/shard_map/rtij,rtjw->riw/dot_general | solution.py:46
  94.7 0.2 bitcast_subtract_fusion
  94.9 13.4 %all-reduce.1 = bf16[4096,128]{1,0:T(8,128)(2,1)} all-reduce(f32[4096,128]{1,0:T(8,128)S(1)} %bitcast_subtract_fusion), channel_id=1, replica_groups=mesh['grp'=2,'dev'=128] {'grp'}, use_global_device_ids=true, to_apply=%region_2.3 | all-reduce | flops 524288 | bytes 3145728 | tf_op jit(solution)/shard_map/psum | solution.py:57
  (16 shorter events, 0.1 us)
Async XLA Ops:
  0.0 27.7 %copy-start = (bf16[1024,128]{1,0:T(8,128)(2,1)S(1)}, bf16[1024,128]{1,0:T(8,128)(2,1)}, u32[]{:S(2)}) copy-start(bf16[1024,128]{1,0:T(8,128)(2,1)} %param.7) | copy-start | bytes 786436
  27.7 14.1 %copy-start.3 = (s32[1,1,2048]{2,1,0:T(1,128)S(1)}, s32[1,1,2048]{2,1,0:T(1,128)}, u32[]{:S(2)}) copy-start(s32[1,1,2048]{2,1,0:T(1,128)} %param.9) | copy-start | bytes 24580
  27.7 14.7 %copy-start.4 = (s32[32,1,8]{0,2,1:T(8,128)S(1)}, s32[32,1,8]{0,2,1:T(8,128)}, u32[]{:S(2)}) copy-start(s32[32,1,8]{0,2,1:T(8,128)} %param.11) | copy-start | bytes 3076
  35.0 24.5 %all-to-all-start.1 = ((bf16[128,1,1,16,128]{4,3,2,1,0:T(8,128)(2,1)}), bf16[128,1,1,16,128]{4,3,2,1,0:T(8,128)(2,1)S(1)}, u32[]{:S(2)}, u32[]{:S(2)}) async-start(bf16[128,1,1,16,128]{4,3,2,1,0:T(8,128)(2,1)} %broadcast_select_fusion), calls=%async_computation.1 | async-start | bytes 1048576 | tf_op jit(solution)/shard_map/all_to_all | solution.py:30
  63.2 10.6 %collective-permute-start = (bf16[2048,128]{1,0:T(8,128)(2,1)S(1)}, bf16[2048,128]{1,0:T(8,128)(2,1)S(1)}, u32[]{:S(2)}, u32[]{:S(2)}) collective-permute-start(bf16[2048,128]{1,0:T(8,128)(2,1)S(1)} %bitcast.45), channel_id=1, source_target_pairs={{0,1},{1,2},{2,3},{3,4},{4,5},{5,6},{6,7},{7,8},{8,9},{9,10},{10,1... | collective-permute-start | bytes 1572872 | tf_op jit(solution)/shard_map/ppermute | solution.py:14
  65.7 12.0 %collective-permute-start.1 = (bf16[2048,128]{1,0:T(8,128)(2,1)S(1)}, bf16[2048,128]{1,0:T(8,128)(2,1)S(1)}, u32[]{:S(2)}, u32[]{:S(2)}) collective-permute-start(bf16[2048,128]{1,0:T(8,128)(2,1)S(1)} %bitcast.46), channel_id=1, source_target_pairs={{1,0},{2,1},{3,2},{4,3},{5,4},{6,5},{7,6},{8,7},{9,8},{10,9},{11,1... | collective-permute-start | bytes 1572872 | tf_op jit(solution)/shard_map/ppermute | solution.py:15
  67.3 6.6 %copy-start.1 = (f32[4096,128]{1,0:T(8,128)}, f32[4096,128]{1,0:T(8,128)S(1)}, u32[]{:S(2)}) copy-start(f32[4096,128]{1,0:T(8,128)S(1)} %convert_dynamic-update-slice_fusion) | copy-start | bytes 6291460
  86.4 8.3 %copy-start.2 = (f32[4096,128]{1,0:T(8,128)S(1)}, f32[4096,128]{1,0:T(8,128)}, u32[]{:S(2)}) copy-start(f32[4096,128]{1,0:T(8,128)} %copy-done.1) | copy-start | bytes 6291460
where the time goes:
time: 109 us; the launch traced here: 108 us
  blocking collectives  40.1 us (37%)
  waiting for transfers between devices  27.4 us (25%)
  local copies, waits for them, and re-layouts  16.6 us (15%)
  matrix products  11.9 us (11%)
  starting transfers between devices  9.97 us (9%)
  other arithmetic  2.15 us (2%)
    all_to_all x1, blocking collectives, per_device(): lax.all_to_all(req_ids, 'dev', split_axis=2, concat_axis=0, tiled=True)  26.7 us
    all_to_all x1, waiting for transfers between devices, per_device(): lax.all_to_all(wanted_rows, 'dev', split_axis=0, concat_axis=2, tiled=True)  17 us
    psum x1, blocking collectives, per_device(): summed = lax.psum(partial_value, 'grp')  13.4 us
    gather x1, local copies, waits for them, and re-layouts, per_device(): picked = ext_blocks[tile_cols[:, 0, :]]  8.61 us
    dot_general x1, matrix products, per_device(): jnp.einsum('rtij,rtjw->riw', tiles[:, 0], picked, preferred_element_type=...  8.25 us
    ppermute x1, waiting for transfers between devices, with_halo(): before = lax.ppermute(last, axis, up)  6.57 us
    gather x1, local copies, waits for them, and re-layouts, per_device(): jnp.take(coarse_emb, lax.all_to_all(req_ids, 'dev', split_axis=2, concat_...  6.19 us
    all_to_all x1, starting transfers between devices, per_device(): lax.all_to_all(wanted_rows, 'dev', split_axis=0, concat_axis=2, tiled=True)  6.18 us
  transfers between devices with their start and end apart: 3, of which 3 were waited for; matrix products, arithmetic and copies ran while one was open for 1% of the time, Pallas kernels for 0%

commit v1 on v0

--- a/solution.py
+++ b/solution.py
@@ -54,7 +54,7 @@
         (group * half_rows, 0),
     )
     partial_value = own_part - 0.5 * tile_sums
-    summed = lax.psum(partial_value, "grp")
+    summed = jnp.sum(lax.all_gather(partial_value, "grp"), axis=0)
     return summed.astype(jnp.bfloat16)
 
 

time: 109 us -> 138 us (1.27)
  waiting for transfers between devices: 27.4 us -> 50.8 us
  between operations: 0.18 us -> 13.6 us
  blocking collectives: 40.1 us -> 26.7 us
  other arithmetic: 2.15 us -> 7.37 us
    all_gather x0 -> x1, waiting for transfers between devices: none -> 23.8 us  [per_device(): summed = jnp.sum(lax.all_gather(partial_value, 'grp'), axis=0)]
    psum x1 -> x0, blocking collectives: 13.4 us -> none  [per_device(): summed = lax.psum(partial_value, 'grp')]
    reduce_sum x0 -> x1, other arithmetic: none -> 3.77 us  [per_device(): summed = jnp.sum(lax.all_gather(partial_value, 'grp'), axis=0)]
  transfers between devices with their start and end apart: 3 -> 4, of which waited for: 3 -> 4; matrix products, arithmetic and copies ran while one was open for 1% -> 1% of each run, Pallas kernels for 0% -> 0%
where the time goes in v1:
time: 138 us; the launch traced here: 137 us
  waiting for transfers between devices  50.8 us (37%)
  blocking collectives  26.7 us (19%)
  local copies, waits for them, and re-layouts  16.7 us (12%)
  between operations  13.6 us (10%)
  matrix products  11.9 us (9%)
  starting transfers between devices  10.2 us (7%)
  other arithmetic  7.37 us (5%)
    all_to_all x1, blocking collectives, per_device(): lax.all_to_all(req_ids, 'dev', split_axis=2, concat_axis=0, tiled=True)  26.7 us
    all_gather x1, waiting for transfers between devices, per_device(): summed = jnp.sum(lax.all_gather(partial_value, 'grp'), axis=0)  23.8 us
    all_to_all x1, waiting for transfers between devices, per_device(): lax.all_to_all(wanted_rows, 'dev', split_axis=0, concat_axis=2, tiled=True)  16.7 us
    gather x1, local copies, waits for them, and re-layouts, per_device(): picked = ext_blocks[tile_cols[:, 0, :]]  8.63 us
    dot_general x1, matrix products, per_device(): jnp.einsum('rtij,rtjw->riw', tiles[:, 0], picked, preferred_element_type=...  8.25 us
    ppermute x1, waiting for transfers between devices, with_halo(): before = lax.ppermute(last, axis, up)  6.39 us
    gather x1, local copies, waits for them, and re-layouts, per_device(): jnp.take(coarse_emb, lax.all_to_all(req_ids, 'dev', split_axis=2, concat_...  6.19 us
    all_to_all x1, starting transfers between devices, per_device(): lax.all_to_all(wanted_rows, 'dev', split_axis=0, concat_axis=2, tiled=True)  6.18 us
  transfers between devices with their start and end apart: 4, of which 4 were waited for; matrix products, arithmetic and copies ran while one was open for 1% of the time, Pallas kernels for 0%

profile of v1, /device:TPU:1, one launch (start us, length us, event | category | flops | bytes accessed | tf_op | source)
XLA Modules:
  0.0 137.2 jit_solution(17537411295098364948)
XLA Ops:
  6.5 0.8 copy.10
  7.4 26.7 %all_to_all.24 = s32[1,1,128,16]{3,1,0,2:T(1,128)S(1)} all-to-all(s32[1,1,128,16]{3,1,0,2:T(1,128)S(1)} %copy.10), channel_id=1, replica_groups=mesh['grp'=2,'dev'=128] {'dev'}, dimensions={2} | all-to-all | bytes 16384 | tf_op jit(solution)/shard_map/all_to_all | solution.py:28
  34.1 0.1 reshape.137
  34.2 0.0 copy-start.3
  34.2 0.0 copy-start.4
  34.3 6.2 %gather_fusion = bf16[2048,128]{1,0:T(8,128)(2,1)S(1)} fusion(bf16[1024,128]{1,0:T(8,128)(2,1)S(1)} %copy-done, s32[2048]{0:T(1024)S(1)} %broadcast_clamp_fusion), kind=kCustom, calls=%fused_computation | custom fusion | bytes 1056768 | tf_op jit(solution)/shard_map/jit(_take)/gather | solution.py:27
  40.4 1.1 broadcast_select_fusion
  41.6 6.2 %all-to-all-start.1 = ((bf16[128,1,1,16,128]{4,3,2,1,0:T(8,128)(2,1)}), bf16[128,1,1,16,128]{4,3,2,1,0:T(8,128)(2,1)S(1)}, u32[]{:S(2)}, u32[]{:S(2)}) async-start(bf16[128,1,1,16,128]{4,3,2,1,0:T(8,128)(2,1)} %broadcast_select_fusion), calls=%async_computation.1 | async-start | bytes 1048576 | tf_op jit(solution)/shard_map/all_to_all | solution.py:30
  47.8 0.0 all-gather.3.cloned.1.call-start
  47.8 0.6 broadcast.89
  48.4 0.7 reduce.3
  49.2 0.1 copy.12
  49.2 0.1 reshape.145
  49.3 16.7 %all-to-all-done.1 = bf16[128,1,1,16,128]{4,3,2,1,0:T(8,128)(2,1)S(1)} async-done(((bf16[128,1,1,16,128]{4,3,2,1,0:T(8,128)(2,1)}), bf16[128,1,1,16,128]{4,3,2,1,0:T(8,128)(2,1)S(1)}, u32[]{:S(2)}, u32[]{:S(2)}) %all-to-all-start.1) | async-done | bytes 524320 | tf_op jit(solution)/shard_map/all_to_all | solution.py:30
  66.0 3.7 %while.11 = (s32[]{:T(128)}, bf16[4,512,128]{2,1,0:T(8,128)(2,1)S(1)}, s32[4,512]{1,0:T(4,128)S(1)}, bf16[2048,128]{1,0:T(8,128)(2,1)S(1)}, s32[]{:T(128)}) while((s32[]{:T(128)}, bf16[4,512,128]{2,1,0:T(8,128)(2,1)S(1)}, s32[4,512]{1,0:T(4,128)S(1)}, bf16[2048,128]{1,0:T(8,128)(2,1)S(1)}, s32[]{:T(128)}) %tuple.26), condition=%wide.region_1.2_spmd.clone, body=%wide.region_0.1_spmd.clone.sunk | while | flops 269549568 | bytes 661573 | solution.py:40
  66.0 0.9 fusion.16
  67.0 0.9 fusion.16
  67.9 0.9 fusion.16
  68.8 0.9 fusion.16
  69.8 2.5 %collective-permute-start = (bf16[2048,128]{1,0:T(8,128)(2,1)S(1)}, bf16[2048,128]{1,0:T(8,128)(2,1)S(1)}, u32[]{:S(2)}, u32[]{:S(2)}) collective-permute-start(bf16[2048,128]{1,0:T(8,128)(2,1)S(1)} %bitcast.47), channel_id=1, source_target_pairs={{0,1},{1,2},{2,3},{3,4},{4,5},{5,6},{6,7},{7,8},{8,9},{9,10},{10,1... | collective-permute-start | bytes 1572872 | tf_op jit(solution)/shard_map/ppermute | solution.py:14
  72.3 1.5 %collective-permute-start.1 = (bf16[2048,128]{1,0:T(8,128)(2,1)S(1)}, bf16[2048,128]{1,0:T(8,128)(2,1)S(1)}, u32[]{:S(2)}, u32[]{:S(2)}) collective-permute-start(bf16[2048,128]{1,0:T(8,128)(2,1)S(1)} %bitcast.48), channel_id=1, source_target_pairs={{1,0},{2,1},{3,2},{4,3},{5,4},{6,5},{7,6},{8,7},{9,8},{10,9},{11,1... | collective-permute-start | bytes 1572872 | tf_op jit(solution)/shard_map/ppermute | solution.py:15
  73.8 0.1 broadcast_in_dim.23
  73.9 0.1 convert_dynamic-update-slice_fusion
  74.0 6.4 %collective-permute-done = bf16[2048,128]{1,0:T(8,128)(2,1)S(1)} collective-permute-done((bf16[2048,128]{1,0:T(8,128)(2,1)S(1)}, bf16[2048,128]{1,0:T(8,128)(2,1)S(1)}, u32[]{:S(2)}, u32[]{:S(2)}) %collective-permute-start) | collective-permute-done | bytes 524320 | tf_op jit(solution)/shard_map/ppermute | solution.py:14
  80.4 3.9 %collective-permute-done.1 = bf16[2048,128]{1,0:T(8,128)(2,1)S(1)} collective-permute-done((bf16[2048,128]{1,0:T(8,128)(2,1)S(1)}, bf16[2048,128]{1,0:T(8,128)(2,1)S(1)}, u32[]{:S(2)}, u32[]{:S(2)}) %collective-permute-start.1) | collective-permute-done | bytes 524320 | tf_op jit(solution)/shard_map/ppermute | solution.py:15
  84.2 0.1 pad_maximum_fusion
  84.4 8.6 %gather_fusion.1 = bf16[256,128,128]{2,1,0:T(8,128)(2,1)} fusion(bf16[48,128,128]{2,1,0:T(8,128)(2,1)S(1)} %bitcast.43, s32[1024]{0:T(1024)S(1)} %pad_clamp_fusion), kind=kCustom, calls=%fused_computation.1 | custom fusion | bytes 16778240 | tf_op jit(solution)/shard_map/gather | solution.py:45
  93.0 8.3 %bitcast_multiply_fusion = f32[32,128,128]{1,2,0:T(8,128)S(1)} fusion(bf16[32,8,128,128]{3,2,1,0:T(8,128)(2,1)} %bitcast.44, bf16[32,1,8,128,128]{4,3,2,1,0:T(8,128)(2,1)} %param.10), kind=kOutput, calls=%fused_computation.13 | convolution fusion | flops 1074266112 | bytes 18874368 | tf_op jit(solution)/shard_map/rtij,rtjw->riw/dot_general | solution.py:46
  101.3 1.5 %bitcast_subtract_fusion = f32[4096,128]{1,0:T(8,128)} fusion(f32[4096,128]{1,0:T(8,128)S(1)} %copy-done.2, f32[32,128,128]{1,2,0:T(8,128)S(1)} %bitcast_multiply_fusion), kind=kLoop, calls=%fused_computation.12 | loop fusion | flops 524288 | bytes 6291456 | tf_op jit(solution)/shard_map/sub | solution.py:56
  102.8 0.0 all-gather.3.cloned.1.call-update
  102.8 23.8 %all-gather.3.cloned.1.call-done = f32[8192,128]{1,0:T(8,128)} async-done(((f32[4096,128]{1,0:T(8,128)}), f32[8192,128]{1,0:T(8,128)}) %all-gather.3.cloned.1.call-update) | async-done | bytes 4194320 | tf_op jit(solution)/shard_map/all_gather | solution.py:57
  126.6 3.8 %reduce_sum.9 = bf16[4096,128]{1,0:T(8,128)(2,1)} reduce(f32[2,4096,128]{2,1,0:T(8,128)} %bitcast.45, f32[]{:T(128)} %constant.13.clone.1), dimensions={0}, to_apply=%region_2.3 | reduce | flops 524288 | bytes 5242884 | tf_op jit(solution)/shard_map/reduce_sum | solution.py:57
  (19 shorter events, 0.1 us)
Async XLA Ops:
  6.5 27.7 %copy-start = (bf16[1024,128]{1,0:T(8,128)(2,1)S(1)}, bf16[1024,128]{1,0:T(8,128)(2,1)}, u32[]{:S(2)}) copy-start(bf16[1024,128]{1,0:T(8,128)(2,1)} %param.7) | copy-start | bytes 786436
  34.2 14.2 %copy-start.3 = (s32[1,1,2048]{2,1,0:T(1,128)S(1)}, s32[1,1,2048]{2,1,0:T(1,128)}, u32[]{:S(2)}) copy-start(s32[1,1,2048]{2,1,0:T(1,128)} %param.9) | copy-start | bytes 24580
  34.2 14.9 %copy-start.4 = (s32[32,1,8]{0,2,1:T(8,128)S(1)}, s32[32,1,8]{0,2,1:T(8,128)}, u32[]{:S(2)}) copy-start(s32[32,1,8]{0,2,1:T(8,128)} %param.11) | copy-start | bytes 3076
  41.6 24.5 %all-to-all-start.1 = ((bf16[128,1,1,16,128]{4,3,2,1,0:T(8,128)(2,1)}), bf16[128,1,1,16,128]{4,3,2,1,0:T(8,128)(2,1)S(1)}, u32[]{:S(2)}, u32[]{:S(2)}) async-start(bf16[128,1,1,16,128]{4,3,2,1,0:T(8,128)(2,1)} %broadcast_select_fusion), calls=%async_computation.1 | async-start | bytes 1048576 | tf_op jit(solution)/shard_map/all_to_all | solution.py:30
  47.8 78.8 %all-gather.3.cloned.1.call-start = ((), (), s32[]{:S(2)}) async-start(), calls=%async_computation.2 | async-start | bytes 6291456 | tf_op jit(solution)/shard_map/all_gather | solution.py:57
  69.8 10.6 %collective-permute-start = (bf16[2048,128]{1,0:T(8,128)(2,1)S(1)}, bf16[2048,128]{1,0:T(8,128)(2,1)S(1)}, u32[]{:S(2)}, u32[]{:S(2)}) collective-permute-start(bf16[2048,128]{1,0:T(8,128)(2,1)S(1)} %bitcast.47), channel_id=1, source_target_pairs={{0,1},{1,2},{2,3},{3,4},{4,5},{5,6},{6,7},{7,8},{8,9},{9,10},{10,1... | collective-permute-start | bytes 1572872 | tf_op jit(solution)/shard_map/ppermute | solution.py:14
  72.3 12.0 %collective-permute-start.1 = (bf16[2048,128]{1,0:T(8,128)(2,1)S(1)}, bf16[2048,128]{1,0:T(8,128)(2,1)S(1)}, u32[]{:S(2)}, u32[]{:S(2)}) collective-permute-start(bf16[2048,128]{1,0:T(8,128)(2,1)S(1)} %bitcast.48), channel_id=1, source_target_pairs={{1,0},{2,1},{3,2},{4,3},{5,4},{6,5},{7,6},{8,7},{9,8},{10,9},{11,1... | collective-permute-start | bytes 1572872 | tf_op jit(solution)/shard_map/ppermute | solution.py:15
  74.0 6.4 %copy-start.1 = (f32[4096,128]{1,0:T(8,128)}, f32[4096,128]{1,0:T(8,128)S(1)}, u32[]{:S(2)}) copy-start(f32[4096,128]{1,0:T(8,128)S(1)} %convert_dynamic-update-slice_fusion) | copy-start | bytes 6291460
  93.0 8.3 %copy-start.2 = (f32[4096,128]{1,0:T(8,128)S(1)}, f32[4096,128]{1,0:T(8,128)}, u32[]{:S(2)}) copy-start(f32[4096,128]{1,0:T(8,128)} %copy-done.1) | copy-start | bytes 6291460
Sparse Core Ops, SparseCore 0:
  102.9 23.6 all-gather.2
